TPU v7x, 32 devices: a whole 2x2x4 slice. The times are simulated.
32 devices in a mesh: groups: 2 (over y), store: 4 (over z), head: 2 (over x), sub: 2 (over core).
Axes of the slice: x: 2, y: 2, z: 4, core: 2. Of those that a mesh axis runs over, the one named last changes fastest.
Arguments:
- fresh_query: bfloat16 [16, 528, 8192], P(('groups', 'store'), None, ('head', 'sub')), parts along dimension 0, may hold values from -20 to 20
- fresh_keys: bfloat16 [16, 528, 1024], P(('groups', 'store'), None, 'head'), parts along dimension 0, may hold values from -6 to 6
- fresh_values: bfloat16 [16, 528, 1024], P(('groups', 'store'), None, 'head'), parts along dimension 0, may hold values from -24 to 24
- store_keys: bfloat16 [64, 512, 1024], P(('groups', 'store'), 'sub', 'head'), parts along dimension 0, may hold values from -6 to 6
- store_values: bfloat16 [64, 512, 1024], P(('groups', 'store'), 'sub', 'head'), parts along dimension 0, may hold values from -24 to 24
- span_ids: int32 [16, 6], P('groups'), parts along dimension 0, may hold values from 0 to 31, as said below
- span_slot: int32 [64], P('groups'), parts along dimension 0, may hold values from 0 to 31, as said below
- select_pos: int32 [16, 464], P('groups'), parts along dimension 0, may hold values from 0 to 3071, as said below
- ask_len: int32 [16], P('groups'), parts along dimension 0, may hold values from 1 to 64, as said below
Outputs:
- attn_out: bfloat16 [16, 528, 8192], P(('groups', 'store'), None, ('head', 'sub')), parts along dimension 0
There are 2 independent parts, one for each index of `groups`. A program takes and returns all parts, laid end to end along the dimension named above; each array names one. Nothing has to cross between parts.
Inputs may be any that keep to these rules, and one draw needn't show every extreme that they name: `span_ids`: the 6 spans of a request are distinct. Over the 2 requests of one store index (requests s * 2 to s * 2 + 1) all named spans are distinct, and at most 3 of them have slots on any one store index, exactly 3 on some. `span_slot`: A permutation; the span with slot v is held by store index v // 8. `select_pos`: strictly increasing within each request. `ask_len`: some request has 64.
All inputs are finite; a program needn't handle non-finite values.
Results may differ from a plain program's by a relative error of at most 0.0045.
Values may be sent and summed in bfloat16 or wider, within the bound.
No kernel may reach another device: no remote copies, remote signals or barrier semaphores. Data moves between devices by JAX's collectives and lax.ppermute only.
A program may use at most 128 MiB of HBM per device.

v0:
```python
import functools
import math

import jax
import jax.numpy as jnp
from jax import lax
from jax.experimental import pallas as pl
from jax.experimental.pallas import tpu as pltpu
from jax.sharding import PartitionSpec as P


HD = 128
GROUP = 8
SPAN = 512
NCH = 6
CTX = 3072
SEL = 464
QLEN = 64
ROWS = 528

NEGATIVE = -1e30
LIMIT = 108.0
TILE = 48
LOG_SCALE = HD ** (-0.5) * math.log2(math.e)


class Plan:
    def __init__(self, fresh_query, store_keys, span_ids):
        self.stores = lax.axis_size("store")
        self.cores = lax.axis_size("sub")
        self.req_dev = fresh_query.shape[0]
        self.ch_dev, self.half, self.kv_columns = store_keys.shape
        self.refs = self.req_dev * NCH
        self.capacity = (self.refs + self.stores - 1) // self.stores
        self.q_columns = fresh_query.shape[2]
        self.q_heads = self.q_columns // HD
        self.kv_used = max(self.q_heads // GROUP, 1)
        self.per_kv = self.q_heads // self.kv_used
        self.width = self.kv_used * HD
        self.reqs = span_ids.shape[0]
        self.source_rows = self.capacity * self.half
        self.sent_rows = self.source_rows
        self.chunks = ((0, self.sent_rows),)
        self.split = self.chunks
        if self.capacity > 1:
            first = (self.capacity - 1) * self.half
            self.split = ((0, first), (first, self.sent_rows - first))
        self.kv_block = lax.div(lax.axis_index("sub") * self.q_heads, GROUP * self.kv_used)

    def kv_start(self, core):
        return pl.multiple_of(lax.div(core * self.q_heads, GROUP) * HD, HD)

    def partner(self, store, step):
        if self.stores & (self.stores - 1) == 0:
            return store ^ step
        return lax.rem(store + step, self.stores)

    def origin(self, store, step):
        if self.stores & (self.stores - 1) == 0:
            return store ^ step
        return lax.rem(store + self.stores - step, self.stores)

    def pairs(self, step, turn):
        listed = []
        for store in range(self.stores):
            for core in range(self.cores):
                if self.stores & (self.stores - 1) == 0:
                    other = store ^ step
                else:
                    other = (store + step) % self.stores
                listed.append((store * self.cores + core, other * self.cores + (core + turn) % self.cores))
        return listed


def find_spans(plan, ids_ref, slot_ref, source, dest):
    zero = jnp.int32(0)
    places, owners, turns, live = ([zero] * plan.capacity for _ in range(4))
    seen = zero
    for turn in range(NCH):
        for request in range(plan.req_dev):
            slot = slot_ref[ids_ref[(dest * plan.req_dev + request) * NCH + turn]]
            place = slot - source * plan.ch_dev
            hit = (place >= 0) & (place < plan.ch_dev)
            for rank in range(plan.capacity):
                here = hit & (seen == rank)
                places[rank] = jnp.where(here, place, places[rank])
                owners[rank] = jnp.where(here, request, owners[rank])
                turns[rank] = jnp.where(here, turn, turns[rank])
                live[rank] = jnp.where(here, 1, live[rank])
            seen = seen + hit.astype(jnp.int32)
    return places, owners, turns, live


def live_ranks(plan, chosen_ref, dest, core, owners, turns, live):
    lane_request = lax.broadcasted_iota(jnp.int32, chosen_ref.shape, 1)
    lane = lax.broadcasted_iota(jnp.int32, (SEL, plan.half), 1)
    before = (
        lax.broadcasted_iota(jnp.int32, (plan.half, plan.half), 0)
        < lax.broadcasted_iota(jnp.int32, (plan.half, plan.half), 1)
    ).astype(jnp.bfloat16)
    sent = jnp.zeros((1, 1), jnp.float32)
    ranks = []
    for rank in range(plan.capacity):
        request = dest * plan.req_dev + owners[rank]
        column = jnp.sum(jnp.where(lane_request == request, chosen_ref[...], 0), axis=1, keepdims=True)
        base = turns[rank] * SPAN + core * plan.half
        hits = jnp.where(column - base == lane, 1.0, 0.0)
        keep = (1.0 - jnp.sum(hits, axis=0, keepdims=True)) * live[rank].astype(jnp.float32)
        ahead = jnp.dot(
            jnp.broadcast_to(keep, (16, plan.half)).astype(jnp.bfloat16), before,
            preferred_element_type=jnp.float32,
        )[:1]
        ranks.append(jnp.where(keep > 0.5, ahead + sent, -1.0))
        sent = sent + jnp.sum(keep, axis=1, keepdims=True)
    return jnp.concatenate(ranks, axis=1).astype(jnp.int32)


def selection(ranks, row_first, rows):
    wanted = lax.broadcasted_iota(jnp.int32, (rows, ranks.shape[1]), 0) + row_first
    return jnp.where(wanted == ranks, 1.0, 0.0).astype(jnp.bfloat16)


def pack_kernel(plan, step, chunks, ids_ref, slot_ref, chosen_ref, keys_ref, values_ref, *rest):
    outs, (key_rows, value_rows, sems) = rest[: -3], rest[-3:]
    store, core = lax.axis_index("store"), lax.axis_index("sub")
    dest = plan.partner(store, step)
    places, owners, turns, live = find_spans(plan, ids_ref, slot_ref, store, dest)
    copies = []
    for rank in range(plan.capacity):
        rows = pl.ds(rank * plan.half, plan.half)
        copies.append(pltpu.make_async_copy(keys_ref.at[places[rank]], key_rows.at[rows], sems.at[0, rank]))
        copies.append(pltpu.make_async_copy(values_ref.at[places[rank]], value_rows.at[rows], sems.at[1, rank]))
    for copy in copies:
        copy.start()
    ranks = live_ranks(plan, chosen_ref, dest, core, owners, turns, live)
    for copy in copies:
        copy.wait()
    for row_first, rows in tiles(plan.sent_rows):
        first = row_first // plan.half * plan.half
        select = selection(ranks[:, first:], row_first, rows)
        for turn in range(plan.cores):
            start = plan.kv_start(lax.rem(core + turn, plan.cores))
            for number, (chunk_first, chunk_rows) in enumerate(chunks):
                if chunk_first <= row_first < chunk_first + chunk_rows:
                    out = outs[number * plan.cores + turn]
                    place = slice(row_first - chunk_first, row_first - chunk_first + rows)
            for source, offset in ((key_rows, 0), (value_rows, plan.width)):
                out[place, offset : offset + plan.width] = jnp.dot(
                    select, source[first:, pl.ds(start, plan.width)], preferred_element_type=jnp.float32
                ).astype(jnp.bfloat16)


def tiles(rows, size=256):
    return [(first, min(size, rows - first)) for first in range(0, rows, size)]


def pack(plan, step, chunks, ids, slots, chosen, store_keys, store_values):
    shapes = [
        jax.ShapeDtypeStruct((rows, 2 * plan.width), jnp.bfloat16)
        for _, rows in chunks
        for _ in range(plan.cores)
    ]
    return pl.pallas_call(
        functools.partial(pack_kernel, plan, step, chunks),
        out_shape=shapes,
        grid_spec=pltpu.PrefetchScalarGridSpec(
            num_scalar_prefetch=2,
            grid=(1,),
            in_specs=[
                pl.BlockSpec(chosen.shape, lambda i, *_: (0, 0)),
                pl.BlockSpec(memory_space=pl.ANY),
                pl.BlockSpec(memory_space=pl.ANY),
            ],
            out_specs=[pl.BlockSpec(s.shape, lambda i, *_: (0, 0)) for s in shapes],
            scratch_shapes=[
                pltpu.VMEM((plan.source_rows, plan.kv_columns), jnp.bfloat16),
                pltpu.VMEM((plan.source_rows, plan.kv_columns), jnp.bfloat16),
                pltpu.SemaphoreType.DMA((2, plan.capacity)),
            ],
        ),
        cost_estimate=pl.CostEstimate(
            flops=4 * plan.source_rows**2 * plan.kv_columns,
            bytes_accessed=8 * plan.source_rows * plan.kv_columns,
            transcendentals=0,
        ),
    )(ids, slots, chosen, store_keys, store_values)


def spans_before(position_row, start):
    return jnp.sum(jnp.where(position_row < start, 1.0, 0.0), axis=1, keepdims=True)


def blend(plan, stage, table, my_pos_ref, fresh_key_ref, fresh_value_ref, streams, keys, values):
    core = lax.axis_index("sub")
    for turn in range(plan.cores):
        source_core = lax.rem(core + plan.cores - turn, plan.cores)
        offset = jnp.zeros((1, 1), jnp.float32)
        for rank in range(max(stage.ranks) + 1):
            owner, base = table[2 * rank], table[2 * rank + 1] + source_core * plan.half
            live = owner >= 0
            request = jnp.maximum(owner, 0)
            listed = my_pos_ref[pl.ds(request, 1), :]
            first = spans_before(listed, base)
            taken = spans_before(listed, base + plan.half) - first
            if rank in stage.ranks:
                at = stage.ranks.index(rank)

                @pl.when(live)
                def _(at=at, offset=offset, first=first, listed=listed, base=base, request=request):
                    token = lax.broadcasted_iota(jnp.int32, (plan.half, SEL), 0) + base
                    same = jnp.where(listed == token, 1.0, 0.0)
                    ahead = jnp.sum(jnp.where(listed < token, 1.0, 0.0), axis=1, keepdims=True)
                    chosen = jnp.sum(same, axis=1, keepdims=True)
                    row = lax.broadcasted_iota(jnp.int32, (plan.half, 1), 0).astype(jnp.float32)
                    row = row + offset - ahead + first
                    row = jnp.where(chosen > 0.5, -1.0, row).astype(jnp.int32)
                    fresh_pick = same.astype(jnp.bfloat16)
                    key = jnp.dot(fresh_pick, fresh_key_ref[request, :SEL, :], preferred_element_type=jnp.float32)
                    value = jnp.dot(fresh_pick, fresh_value_ref[request, :SEL, :], preferred_element_type=jnp.float32)
                    if len(stage.chunks) == 1 and plan.sent_rows >= plan.half + 16:
                        rows = plan.half + 16
                        below = jnp.max(offset.astype(jnp.int32)) // 16 * 16
                        below = pl.multiple_of(jnp.minimum(below, plan.sent_rows - rows), 16)
                        parts = [(below, rows, streams[turn], pl.ds(below, rows))]
                    else:
                        parts = [
                            (first_row, rows, streams[number * plan.cores + turn], slice(None))
                            for number, (first_row, rows) in enumerate(stage.chunks)
                        ]
                    for first_row, rows, stream, window in parts:
                        lane = lax.broadcasted_iota(jnp.int32, (plan.half, rows), 1) + first_row
                        pick = jnp.where(lane == row, 1.0, 0.0).astype(jnp.bfloat16)
                        both = jnp.dot(pick, stream[window, :], preferred_element_type=jnp.float32)
                        key = key + both[:, : plan.width]
                        value = value + both[:, plan.width :]
                    place = pl.ds(pl.multiple_of(source_core * plan.half, plan.half), plan.half)
                    keys[at, place, :] = key.astype(jnp.bfloat16)
                    values[at, place, :] = value.astype(jnp.bfloat16)

            offset = offset + (plan.half - taken) * live.astype(jnp.float32)


def attend_kernel(plan, stage, *refs):
    refs = list(refs)

    def take(count):
        taken = refs[:count]
        del refs[:count]
        return taken

    ids_ref, slot_ref, pos_ref, len_ref, _ = take(5)
    column_ref, my_pos_ref, fresh_key_ref, fresh_value_ref = take(4)
    if stage.opening:
        (query_in,) = take(1)
    else:
        query, sizes = take(2)
        take(3)
    streams = take(len(stage.chunks) * plan.cores)
    if stage.closing:
        (out_ref,) = take(1)
    total_ref, sums_ref, top_ref = take(3)
    if stage.opening:
        query, sizes = take(2)
    keys, values, table = take(3)
    request = pl.program_id(0)
    store = lax.axis_index("store")
    span = plan.half * plan.cores
    last = ROWS // TILE
    bunch = plan.per_kv * TILE

    @pl.when(request == 0)
    def _():
        source = plan.origin(store, stage.step)
        _, owners, turns, live = find_spans(plan, ids_ref, slot_ref, source, store)
        for rank in range(plan.capacity):
            table[2 * rank] = jnp.where(live[rank] > 0, owners[rank], -1)
            table[2 * rank + 1] = turns[rank] * SPAN
        blend(plan, stage, table, my_pos_ref, fresh_key_ref, fresh_value_ref, streams, keys, values)

    def rows_of(tile):
        return pl.ds(pl.multiple_of(tile * TILE, 16), TILE)

    def bunch_of(tile, count=1):
        return pl.ds(pl.multiple_of(tile * bunch, 16), count * bunch)

    def members():
        for kv in range(plan.kv_used):
            for member in range(plan.per_kv):
                head = kv * plan.per_kv + member
                yield kv, member, slice(head * HD, (head + 1) * HD)

    if stage.opening:
        def prepare(tile, most):
            long, low = most
            for kv, member, lanes in members():
                place = pl.ds(pl.multiple_of(tile * bunch + member * TILE, 16), TILE)
                taken = query_in[0, rows_of(tile), lanes]
                query[request, kv, place, :] = taken
                taken = taken.astype(jnp.float32)
                own = fresh_key_ref[request, rows_of(tile), kv * HD : (kv + 1) * HD].astype(jnp.float32)
                product = jnp.broadcast_to(jnp.sum(taken * own, axis=1, keepdims=True), (TILE, HD))
                top_ref[request, kv, place, :] = product
                total_ref[request, kv, place, :] = jnp.zeros((TILE, HD), jnp.float32)
                sums_ref[request, kv, place, :] = jnp.zeros((TILE, HD), jnp.float32)
                long = jnp.maximum(long, jnp.sum(jnp.abs(taken), axis=1, keepdims=True))
                low = jnp.maximum(low, -product)
            return long, low

        none = jnp.zeros((TILE, HD), jnp.float32)
        long, low = lax.fori_loop(0, last, prepare, (none, none))
        sizes[request, 0] = long
        sizes[request, 1] = low

    def masks(tile, count, width, base):
        lane = lax.broadcasted_iota(jnp.int32, (TILE, width), 1) + base
        return [lane <= column_ref[0, rows_of(tile + more), :] for more in range(count)]

    def quick(tile, count, kv, key, extended, allowed):
        rows = bunch_of(tile, count)
        scores = lax.dot_general(
            query[request, kv, rows, :], key, (((1,), (1,)), ((), ())), preferred_element_type=jnp.float32
        )
        width = key.shape[0] // HD
        powers = []
        for more in range(count):
            for member in range(plan.per_kv):
                first = more * bunch + member * TILE
                place = pl.ds(pl.multiple_of(tile * bunch + first, 16), TILE)
                shift = jnp.concatenate([top_ref[request, kv, place, :]] * width, axis=1)
                power = jnp.exp2((scores[first : first + TILE] - shift) * LOG_SCALE)
                powers.append(jnp.where(allowed[more], power, 0.0).astype(jnp.bfloat16))
        update = jnp.dot(jnp.concatenate(powers, axis=0), extended, preferred_element_type=jnp.float32)
        total_ref[request, kv, rows, :] += update[:, :HD]
        sums_ref[request, kv, rows, :] += update[:, HD:]

    def careful(tile, count, kv, key, extended, allowed):
        def one(number, unused):
            place = pl.ds(pl.multiple_of(tile * bunch + number * TILE, 16), TILE)
            scores = lax.dot_general(
                query[request, kv, place, :], key, (((1,), (1,)), ((), ())), preferred_element_type=jnp.float32
            )
            scores = jnp.where(allowed[0], scores, NEGATIVE)
            old_top = top_ref[request, kv, place, :]
            new_top = jnp.maximum(old_top, jnp.max(scores, axis=1, keepdims=True))
            shift = jnp.concatenate([new_top] * (key.shape[0] // HD), axis=1)
            powers = jnp.exp2((scores - shift) * LOG_SCALE)
            update = jnp.dot(powers.astype(jnp.bfloat16), extended, preferred_element_type=jnp.float32)
            factor = jnp.exp2((old_top - new_top) * LOG_SCALE)
            total_ref[request, kv, place, :] = total_ref[request, kv, place, :] * factor + update[:, :HD]
            sums_ref[request, kv, place, :] = sums_ref[request, kv, place, :] * factor + update[:, HD:]
            top_ref[request, kv, place, :] = new_top
            return unused

        lax.fori_loop(0, plan.per_kv, one, 0)

    def extend(value):
        return jnp.concatenate([value, jnp.ones(value.shape, jnp.bfloat16)], axis=1)

    def last_pos(tile):
        return pos_ref[request * ROWS + (tile + 1) * TILE - 1]

    def run(act, pairs):
        def span_tiles(at, base, tile, count):
            allowed = masks(tile, count, span, base)
            for kv in range(plan.kv_used):
                lanes = slice(kv * HD, (kv + 1) * HD)
                act(tile, count, kv, keys[at, :, lanes], extend(values[at, :, lanes]), allowed)

        def one_span(at, unused):
            rank = at + stage.ranks[0]
            owner, base = table[2 * rank], table[2 * rank + 1]

            @pl.when(owner == request)
            def _():
                if not pairs:
                    def step(tile, unused):
                        span_tiles(at, base, tile, 1)
                        return unused

                    lax.fori_loop(0, last, step, 0)
                    return

                @pl.when(last_pos(0) >= base)
                def _():
                    span_tiles(at, base, 0, 1)

                first = jnp.int32(0)
                for pair in range(last // 2):
                    first = first + (last_pos(2 * pair + 2) < base).astype(jnp.int32)

                def step(pair, unused):
                    span_tiles(at, base, 2 * pair + 1, 2)
                    return unused

                lax.fori_loop(first, last // 2, step, 0)

            return unused

        lax.fori_loop(0, len(stage.ranks), one_span, 0)
        if stage.opening:
            def ask(tile, unused):
                allowed = masks(tile, 1, 2 * QLEN, CTX)
                for kv in range(plan.kv_used):
                    lanes = slice(kv * HD, (kv + 1) * HD)
                    key, value = fresh_key_ref[request, SEL:, lanes], fresh_value_ref[request, SEL:, lanes]
                    key = jnp.concatenate([key, jnp.zeros_like(key)], axis=0)
                    value = jnp.concatenate([value, jnp.zeros_like(value)], axis=0)
                    act(tile, 1, kv, key, extend(value), allowed)
                return unused

            lax.fori_loop(SEL // TILE, last, ask, 0)

    greatest = jnp.max(jnp.abs(keys[...].astype(jnp.float32)))
    if stage.opening:
        greatest = jnp.maximum(greatest, jnp.max(jnp.abs(fresh_key_ref[request].astype(jnp.float32))))
    reach = (greatest * jnp.max(sizes[request, 0]) + jnp.max(sizes[request, 1])) * LOG_SCALE
    held = reach < LIMIT

    @pl.when(held)
    def _():
        run(quick, True)

    @pl.when(jnp.logical_not(held))
    def _():
        run(careful, False)

    if stage.closing:
        def finish(tile, unused):
            row = lax.broadcasted_iota(jnp.int32, (TILE, HD), 0) + tile * TILE
            live = row < SEL + len_ref[request]
            for kv, member, lanes in members():
                place = pl.ds(pl.multiple_of(tile * bunch + member * TILE, 16), TILE)
                result = total_ref[request, kv, place, :] / sums_ref[request, kv, place, :]
                out_ref[0, rows_of(tile), lanes] = jnp.where(live, result, 0.0).astype(jnp.bfloat16)
            return unused

        lax.fori_loop(0, last, finish, 0)


def attend(plan, stage, state, arrays, fresh, ids, slots, my_pos, pos, pos_column, lengths):
    fresh_query, fresh_keys, fresh_values = fresh
    req_dev = plan.req_dev
    row_block = lambda width: pl.BlockSpec((1, ROWS, width), lambda r, *_: (r, 0, 0))
    whole = lambda array: pl.BlockSpec(array.shape, lambda r, *_: (0,) * array.ndim)
    kept = pl.BlockSpec(memory_space=pltpu.VMEM)
    fresh_block = pl.BlockSpec((req_dev, ROWS, plan.width), lambda r, *s: (0, 0, s[4][0]))
    kv_block = jnp.reshape(plan.kv_block, (1,))
    operands = [ids, slots, pos, lengths, kv_block, pos_column, my_pos, fresh_keys, fresh_values]
    specs = [row_block(1), whole(my_pos), fresh_block, fresh_block]
    aliases = {}
    stacked = (req_dev, plan.kv_used, plan.q_heads // plan.kv_used * ROWS, HD)
    out_shape, out_specs = [], []
    if stage.closing:
        out_shape = [jax.ShapeDtypeStruct(fresh_query.shape, jnp.bfloat16)]
        out_specs = [row_block(plan.q_columns)]
    if stage.opening:
        operands.append(fresh_query)
        specs.append(row_block(plan.q_columns))
    else:
        aliases = {len(operands) + 2 + i: len(out_shape) + i for i in range(3)}
        operands += [state[3], state[4], *state[:3]]
        specs += [kept] * 5
    operands += arrays
    specs += [whole(a) for a in arrays]
    span = plan.half * plan.cores
    scratch = [pltpu.VMEM((len(stage.ranks), span, plan.width), jnp.bfloat16)] * 2
    scratch += [pltpu.SMEM((2 * plan.capacity,), jnp.int32)]
    out_shape += [pltpu.VMEM(stacked, jnp.float32)] * 3
    out_specs += [kept] * 3
    if stage.opening:
        out_shape += [pltpu.VMEM(stacked, jnp.bfloat16), pltpu.VMEM((req_dev, 2, TILE, HD), jnp.float32)]
        out_specs += [kept] * 2
    scores = len(stage.ranks) * span * ROWS * plan.q_heads
    result = pl.pallas_call(
        functools.partial(attend_kernel, plan, stage),
        out_shape=out_shape,
        grid_spec=pltpu.PrefetchScalarGridSpec(
            num_scalar_prefetch=5,
            grid=(req_dev,),
            in_specs=specs,
            out_specs=out_specs,
            scratch_shapes=scratch,
        ),
        input_output_aliases=aliases,
        compiler_params=pltpu.CompilerParams(vmem_limit_bytes=20 << 20),
        cost_estimate=pl.CostEstimate(
            flops=4 * scores * HD,
            bytes_accessed=req_dev * ROWS * plan.q_columns * 4,
            transcendentals=scores,
        ),
    )(*operands)
    if stage.closing:
        return result[0]
    return result if stage.opening else list(result) + list(state[3:])


class Stage:
    def __init__(self, step, ranks, chunks, opening=False, closing=False):
        self.step, self.ranks, self.chunks = step, ranks, chunks
        self.opening, self.closing = opening, closing


def body(
    fresh_query,
    fresh_keys,
    fresh_values,
    store_keys,
    store_values,
    span_ids,
    span_slot,
    select_pos,
    ask_len,
):
    plan = Plan(fresh_query, store_keys, span_ids)
    store_index = lax.axis_index("store")
    ids = span_ids.reshape(-1)
    chosen = jnp.transpose(select_pos)
    steps = list(range(1, plan.stores))
    arrived = {}
    for step in steps + [0]:
        chunks = plan.split if step == steps[-1] else plan.chunks
        own_ids = ids
        if step != steps[0]:
            own_ids, _ = lax.optimization_barrier((ids, before))
        packed = pack(plan, step, chunks, own_ids, span_slot, chosen, store_keys, store_values)
        before = packed[0]
        at = 0
        for chunk in range(len(chunks)):
            for turn in range(plan.cores):
                block = packed[at]
                at += 1
                if step != 0 or turn != 0:
                    block = lax.ppermute(block, ("store", "sub"), plan.pairs(step, turn))
                arrived[(step, chunk, turn)] = block
    my_pos = lax.dynamic_slice_in_dim(select_pos, store_index * plan.req_dev, plan.req_dev, 0)
    lengths = lax.dynamic_slice_in_dim(ask_len, store_index * plan.req_dev, plan.req_dev, 0)
    asked = jnp.broadcast_to(CTX + jnp.arange(QLEN, dtype=jnp.int32), (plan.req_dev, QLEN))
    pos = jnp.concatenate([my_pos, asked], axis=1)
    pos_column = pos[:, :, None]
    pos = pos.reshape(-1)
    all_ranks = list(range(plan.capacity))
    stages = [Stage(step, all_ranks, plan.chunks) for step in [0] + steps]
    stages[0].opening = True
    if len(plan.split) > 1:
        stages[-1:] = [
            Stage(steps[-1], all_ranks[:-1], plan.split[:-1]),
            Stage(steps[-1], all_ranks[-1:], plan.split),
        ]
    stages[-1].closing = True
    state = None
    for stage in stages:
        arrays = [
            arrived[(stage.step, chunk, turn)]
            for chunk in range(len(stage.chunks))
            for turn in range(plan.cores)
        ]
        state = attend(
            plan, stage, state, arrays, (fresh_query, fresh_keys, fresh_values), ids, span_slot,
            my_pos, pos, pos_column, lengths,
        )
    return state


def solution(mesh):
    placed = (
        P(("groups", "store"), None, ("head", "sub")),
        P(("groups", "store"), None, "head"),
        P(("groups", "store"), None, "head"),
        P(("groups", "store"), "sub", "head"),
        P(("groups", "store"), "sub", "head"),
        P("groups", None),
        P("groups"),
        P("groups", None),
        P("groups"),
    )
    return jax.shard_map(
        body,
        mesh=mesh,
        in_specs=placed,
        out_specs=P(("groups", "store"), None, ("head", "sub")),
        check_vma=False,
    )
```

profile of v0, /device:TPU:0, one launch (start us, length us, event | category | flops | bytes accessed | tf_op | source)
XLA Modules:
  0.0 1031.4 jit_solution(4004604012928480250)
XLA Ops:
  0.0 1.3 reshape.6.ids_ref.refs_0_
  1.3 1.6 copy.22
  2.9 5.7 shard_map.91
  8.6 5.6 shard_map.92
  14.2 5.4 shard_map.93
  19.7 5.6 shard_map.94
  25.2 0.6 collective-permute-start
  25.8 2.6 collective-permute-start.1
  28.4 2.6 collective-permute-start.3
  31.0 0.1 collective-permute-start.2
  31.3 0.7 constant_dynamic-slice_fusion.refs_6_
  32.0 0.1 reshape.14.refs_2_
  32.1 0.2 copy.27.refs_5_
  32.4 0.9 copy-done.4
  33.2 4.0 collective-permute-start.4
  37.3 1.1 copy-done.5
  38.4 1.1 copy-done.6
  39.5 268.3 %shard_map.95 = (f32[2,2,4224,128]{3,2,1,0:T(8,128)S(1)}, f32[2,2,4224,128]{3,2,1,0:T(8,128)S(1)}, f32[2,2,4224,128]{3,2,1,0:T(8,128)S(1)}, bf16[2,2,4224,128]{3,2,1,0:T(8,128)(2,1)S(1)}, f32[2,2,48,128]{3,2,1,0:T(8,128)S(1)}) custom-call(s32[48]{0:T(128)S(1)} %copy-done.2, s32[32]{0:T(128)S(1)} %copy-done.3, s32[1056]{0:T(1024)S(1)} %reshape.14.refs_2_, ...), custom_call_target="tpu_custom_call" | custom-call | flops 6643777536 | bytes 8650752 | tf_op jit(solution)/shard_map/pallas_call | solution.py:474
  308.0 2.7 collective-permute-start.8
  310.7 238.3 %shard_map.96 = (f32[2,2,4224,128]{3,2,1,0:T(8,128)S(1)}, f32[2,2,4224,128]{3,2,1,0:T(8,128)S(1)}, f32[2,2,4224,128]{3,2,1,0:T(8,128)S(1)}) custom-call(s32[48]{0:T(128)S(1)} %copy-done.2, s32[32]{0:T(128)S(1)} %copy-done.3, s32[1056]{0:T(1024)S(1)} %reshape.14.refs_2_, ...), custom_call_target="tpu_custom_call", output_to_operand_aliasing={{0}: (11, {}), {1}: (12, {}), {2}: (13, {})} | custom-call | flops 6643777536 | bytes 8650752 | tf_op jit(solution)/shard_map/pallas_call | solution.py:474
  549.0 1.0 collective-permute-start.6
  550.0 238.3 %shard_map.97 = (f32[2,2,4224,128]{3,2,1,0:T(8,128)S(1)}, f32[2,2,4224,128]{3,2,1,0:T(8,128)S(1)}, f32[2,2,4224,128]{3,2,1,0:T(8,128)S(1)}) custom-call(s32[48]{0:T(128)S(1)} %copy-done.2, s32[32]{0:T(128)S(1)} %copy-done.3, s32[1056]{0:T(1024)S(1)} %reshape.14.refs_2_, ...), custom_call_target="tpu_custom_call", output_to_operand_aliasing={{0}: (11, {}), {1}: (12, {}), {2}: (13, {})} | custom-call | flops 6643777536 | bytes 8650752 | tf_op jit(solution)/shard_map/pallas_call | solution.py:474
  788.3 159.3 %shard_map.98 = (f32[2,2,4224,128]{3,2,1,0:T(8,128)S(1)}, f32[2,2,4224,128]{3,2,1,0:T(8,128)S(1)}, f32[2,2,4224,128]{3,2,1,0:T(8,128)S(1)}) custom-call(s32[48]{0:T(128)S(1)} %copy-done.2, s32[32]{0:T(128)S(1)} %copy-done.3, s32[1056]{0:T(1024)S(1)} %reshape.14.refs_2_, ...), custom_call_target="tpu_custom_call", output_to_operand_aliasing={{0}: (11, {}), {1}: (12, {}), {2}: (13, {})} | custom-call | flops 4429185024 | bytes 8650752 | tf_op jit(solution)/shard_map/pallas_call | solution.py:474
  947.7 83.7 %shard_map.99 = (bf16[2,528,2048]{2,1,0:T(8,128)(2,1)}, f32[2,2,4224,128]{3,2,1,0:T(8,128)S(1)}, f32[2,2,4224,128]{3,2,1,0:T(8,128)S(1)}, f32[2,2,4224,128]{3,2,1,0:T(8,128)S(1)}) custom-call(s32[48]{0:T(128)S(1)} %copy-done.2, s32[32]{0:T(128)S(1)} %copy-done.3, ...), custom_call_target="tpu_custom_call", output_to_operand_aliasing={{1}: (11, {}), {2}: (12, {}), {3}: (13, {})} | custom-call | flops 2214592512 | bytes 8650752 | tf_op jit(solution)/shard_map/pallas_call | solution.py:474
  (35 shorter events, 0.3 us)
Async XLA Ops:
  2.9 28.3 %copy-start.10 = (s32[8]{0:T(128)S(1)}, s32[8]{0:T(128)}, u32[]{:S(2)}) copy-start(s32[8]{0:T(128)} %param.17) | copy-start | bytes 100
  2.9 34.4 %copy-start = (bf16[2,528,512]{2,1,0:T(8,128)(2,1)S(1)}, bf16[2,528,512]{2,1,0:T(8,128)(2,1)}, u32[]{:S(2)}) copy-start(bf16[2,528,512]{2,1,0:T(8,128)(2,1)} %refs_7_.9) | copy-start | bytes 3244036
  2.9 34.4 %copy-start.1 = (bf16[2,528,512]{2,1,0:T(8,128)(2,1)S(1)}, bf16[2,528,512]{2,1,0:T(8,128)(2,1)}, u32[]{:S(2)}) copy-start(bf16[2,528,512]{2,1,0:T(8,128)(2,1)} %refs_8_.9) | copy-start | bytes 3244036
  2.9 34.4 %copy-start.2 = (s32[48]{0:T(128)S(1)}, s32[48]{0:T(128)}, u32[]{:S(2)}) copy-start(s32[48]{0:T(128)} %reshape.6.ids_ref.refs_0_) | copy-start | bytes 580
  2.9 34.4 %copy-start.3 = (s32[32]{0:T(128)S(1)}, s32[32]{0:T(128)}, u32[]{:S(2)}) copy-start(s32[32]{0:T(128)} %refs_1_.9) | copy-start | bytes 388
  25.2 7.1 collective-permute-start
  25.8 282.2 %collective-permute-start.1 = (bf16[768,512]{1,0:T(8,128)(2,1)}, bf16[768,512]{1,0:T(8,128)(2,1)}, u32[]{:S(2)}, u32[]{:S(2)}) collective-permute-start(bf16[768,512]{1,0:T(8,128)(2,1)} %get-tuple-element.33), channel_id=1, source_target_pairs={{0,4},{1,5},{4,0},{5,1},{8,12},{9,13},{12,8},{13,9},{2,6},{3,7},{6... | collective-permute-start | bytes 2359304 | tf_op jit(solution)/shard_map/ppermute | solution.py:533
  28.4 521.6 %collective-permute-start.3 = (bf16[768,512]{1,0:T(8,128)(2,1)}, bf16[768,512]{1,0:T(8,128)(2,1)}, u32[]{:S(2)}, u32[]{:S(2)}) collective-permute-start(bf16[768,512]{1,0:T(8,128)(2,1)} %get-tuple-element.35), channel_id=1, source_target_pairs={{0,8},{1,9},{4,12},{5,13},{8,0},{9,1},{12,4},{13,5},{2,10},{3,11},... | collective-permute-start | bytes 2359304 | tf_op jit(solution)/shard_map/ppermute | solution.py:533
  31.0 757.3 %collective-permute-start.5 = (bf16[512,512]{1,0:T(8,128)(2,1)}, bf16[512,512]{1,0:T(8,128)(2,1)}, u32[]{:S(2)}, u32[]{:S(2)}) collective-permute-start(bf16[512,512]{1,0:T(8,128)(2,1)} %get-tuple-element.37), channel_id=1, source_target_pairs={{0,12},{1,13},{4,8},{5,9},{8,4},{9,5},{12,0},{13,1},{2,14},{3,15},... | collective-permute-start | bytes 1572872 | tf_op jit(solution)/shard_map/ppermute | solution.py:533
  31.0 276.9 %collective-permute-start.2 = (bf16[768,512]{1,0:T(8,128)(2,1)}, bf16[768,512]{1,0:T(8,128)(2,1)}, u32[]{:S(2)}, u32[]{:S(2)}) collective-permute-start(bf16[768,512]{1,0:T(8,128)(2,1)} %get-tuple-element.46), channel_id=1, source_target_pairs={{0,5},{1,4},{4,1},{5,0},{8,13},{9,12},{12,9},{13,8},{2,7},{3,6},{6... | collective-permute-start | bytes 2359304 | tf_op jit(solution)/shard_map/ppermute | solution.py:533
  32.4 0.9 copy-start.4
  33.2 515.8 %collective-permute-start.4 = (bf16[768,512]{1,0:T(8,128)(2,1)}, bf16[768,512]{1,0:T(8,128)(2,1)S(1)}, u32[]{:S(2)}, u32[]{:S(2)}) collective-permute-start(bf16[768,512]{1,0:T(8,128)(2,1)} %get-tuple-element.50), channel_id=1, source_target_pairs={{0,9},{1,8},{4,13},{5,12},{8,1},{9,0},{12,5},{13,4},{2,11},{3,10},... | collective-permute-start | bytes 2359304 | tf_op jit(solution)/shard_map/ppermute | solution.py:533
  37.3 1.1 copy-start.5
  38.4 1.1 copy-start.6
  39.5 268.4 %copy-start.9 = (bf16[256,512]{1,0:T(8,128)(2,1)S(1)}, bf16[256,512]{1,0:T(8,128)(2,1)}, u32[]{:S(2)}) copy-start(bf16[256,512]{1,0:T(8,128)(2,1)} %get-tuple-element.58) | copy-start | bytes 786436
  39.5 268.5 %copy-start.8 = (bf16[256,512]{1,0:T(8,128)(2,1)S(1)}, bf16[256,512]{1,0:T(8,128)(2,1)}, u32[]{:S(2)}) copy-start(bf16[256,512]{1,0:T(8,128)(2,1)} %get-tuple-element.59) | copy-start | bytes 786436
  307.9 639.7 %collective-permute-start.7 = (bf16[256,512]{1,0:T(8,128)(2,1)S(1)}, bf16[256,512]{1,0:T(8,128)(2,1)S(1)}, u32[]{:S(2)}, u32[]{:S(2)}) collective-permute-start(bf16[256,512]{1,0:T(8,128)(2,1)S(1)} %copy-done.9), channel_id=1, source_target_pairs={{0,12},{1,13},{4,8},{5,9},{8,4},{9,5},{12,0},{13,1},{2,14},{3,15},... | collective-permute-start | bytes 786440 | tf_op jit(solution)/shard_map/ppermute | solution.py:533
  308.0 639.7 %collective-permute-start.8 = (bf16[256,512]{1,0:T(8,128)(2,1)S(1)}, bf16[256,512]{1,0:T(8,128)(2,1)S(1)}, u32[]{:S(2)}, u32[]{:S(2)}) collective-permute-start(bf16[256,512]{1,0:T(8,128)(2,1)S(1)} %copy-done.8), channel_id=1, source_target_pairs={{0,13},{1,12},{4,9},{5,8},{8,5},{9,4},{12,1},{13,0},{2,15},{3,14},... | collective-permute-start | bytes 786440 | tf_op jit(solution)/shard_map/ppermute | solution.py:533
  310.7 238.3 %copy-start.7 = (bf16[512,512]{1,0:T(8,128)(2,1)S(1)}, bf16[512,512]{1,0:T(8,128)(2,1)}, u32[]{:S(2)}) copy-start(bf16[512,512]{1,0:T(8,128)(2,1)} %get-tuple-element.54) | copy-start | bytes 1572868
  549.0 239.2 %collective-permute-start.6 = (bf16[512,512]{1,0:T(8,128)(2,1)S(1)}, bf16[512,512]{1,0:T(8,128)(2,1)S(1)}, u32[]{:S(2)}, u32[]{:S(2)}) collective-permute-start(bf16[512,512]{1,0:T(8,128)(2,1)S(1)} %copy-done.7), channel_id=1, source_target_pairs={{0,13},{1,12},{4,9},{5,8},{8,5},{9,4},{12,1},{13,0},{2,15},{3,14},... | collective-permute-start | bytes 1572872 | tf_op jit(solution)/shard_map/ppermute | solution.py:533
where the time goes:
time: 1030 us
  Pallas kernels  1010 us (98%)
  starting transfers between devices  13.7 us (1%)
    pallas_call x5, Pallas kernels, attend(): pl.pallas_call(functools.partial(attend_kernel, plan, stage), out_shape=o...  988 us
    pallas_call x4, Pallas kernels, pack(): pl.pallas_call(functools.partial(pack_kernel, plan, step, chunks), out_sh...  22.3 us
  transfers between devices with their start and end apart: 9, of which 0 were waited for; matrix products, arithmetic and copies ran while one was open for 0% of the time, Pallas kernels for 88%

commit v1 on v0

--- a/solution.py
+++ b/solution.py
@@ -40,12 +40,25 @@
         self.reqs = span_ids.shape[0]
         self.source_rows = self.capacity * self.half
         self.sent_rows = self.source_rows
-        self.chunks = ((0, self.sent_rows),)
-        self.split = self.chunks
         if self.capacity > 1:
-            first = (self.capacity - 1) * self.half
-            self.split = ((0, first), (first, self.sent_rows - first))
+            part = SEL / CTX
+            likely = self.source_rows * (1 - part) + 3.6 * math.sqrt(self.source_rows * part * (1 - part))
+            likely = -(-math.ceil(likely) // 16) * 16
+            if (self.capacity - 1) * self.half < likely < self.source_rows:
+                self.sent_rows = likely
+        self.left_rows = self.source_rows - self.sent_rows
+
         self.kv_block = lax.div(lax.axis_index("sub") * self.q_heads, GROUP * self.kv_used)
+
+    def chunks(self, step):
+        edges = [0, self.sent_rows]
+        if step == 0:
+            edges = [0, self.source_rows]
+        elif step == self.stores - 1:
+            edges = [rank * self.half for rank in range(self.capacity)] + [self.sent_rows]
+        elif step == self.stores - 2 and self.capacity > 1:
+            edges = [0, (self.capacity - 1) * self.half, self.sent_rows]
+        return [(first, end - first) for first, end in zip(edges[:-1], edges[1:])]
 
     def kv_start(self, core):
         return pl.multiple_of(lax.div(core * self.q_heads, GROUP) * HD, HD)
@@ -135,7 +148,7 @@
     ranks = live_ranks(plan, chosen_ref, dest, core, owners, turns, live)
     for copy in copies:
         copy.wait()
-    for row_first, rows in tiles(plan.sent_rows):
+    for row_first, rows in [tile for chunk in chunks for tile in tiles(*chunk)]:
         first = row_first // plan.half * plan.half
         select = selection(ranks[:, first:], row_first, rows)
         for turn in range(plan.cores):
@@ -150,8 +163,8 @@
                 ).astype(jnp.bfloat16)
 
 
-def tiles(rows, size=256):
-    return [(first, min(size, rows - first)) for first in range(0, rows, size)]
+def tiles(start, rows, size=256):
+    return [(start + first, min(size, rows - first)) for first in range(0, rows, size)]
 
 
 def pack(plan, step, chunks, ids, slots, chosen, store_keys, store_values):
@@ -190,54 +203,59 @@
     return jnp.sum(jnp.where(position_row < start, 1.0, 0.0), axis=1, keepdims=True)
 
 
-def blend(plan, stage, table, my_pos_ref, fresh_key_ref, fresh_value_ref, streams, keys, values):
+def blend(plan, stage, table, left_ref, my_pos_ref, fresh_key_ref, fresh_value_ref, joined, keys, values):
     core = lax.axis_index("sub")
-    for turn in range(plan.cores):
+    held = sum(rows for _, rows in stage.chunks)
+    rows = min(plan.half + 16, held)
+
+    def one_turn(turn, unused):
         source_core = lax.rem(core + plan.cores - turn, plan.cores)
-        offset = jnp.zeros((1, 1), jnp.float32)
-        for rank in range(max(stage.ranks) + 1):
+
+        def one_rank(rank, offset):
             owner, base = table[2 * rank], table[2 * rank + 1] + source_core * plan.half
             live = owner >= 0
             request = jnp.maximum(owner, 0)
             listed = my_pos_ref[pl.ds(request, 1), :]
             first = spans_before(listed, base)
             taken = spans_before(listed, base + plan.half) - first
-            if rank in stage.ranks:
-                at = stage.ranks.index(rank)
-
-                @pl.when(live)
-                def _(at=at, offset=offset, first=first, listed=listed, base=base, request=request):
-                    token = lax.broadcasted_iota(jnp.int32, (plan.half, SEL), 0) + base
-                    same = jnp.where(listed == token, 1.0, 0.0)
-                    ahead = jnp.sum(jnp.where(listed < token, 1.0, 0.0), axis=1, keepdims=True)
-                    chosen = jnp.sum(same, axis=1, keepdims=True)
-                    row = lax.broadcasted_iota(jnp.int32, (plan.half, 1), 0).astype(jnp.float32)
-                    row = row + offset - ahead + first
-                    row = jnp.where(chosen > 0.5, -1.0, row).astype(jnp.int32)
-                    fresh_pick = same.astype(jnp.bfloat16)
-                    key = jnp.dot(fresh_pick, fresh_key_ref[request, :SEL, :], preferred_element_type=jnp.float32)
-                    value = jnp.dot(fresh_pick, fresh_value_ref[request, :SEL, :], preferred_element_type=jnp.float32)
-                    if len(stage.chunks) == 1 and plan.sent_rows >= plan.half + 16:
-                        rows = plan.half + 16
-                        below = jnp.max(offset.astype(jnp.int32)) // 16 * 16
-                        below = pl.multiple_of(jnp.minimum(below, plan.sent_rows - rows), 16)
-                        parts = [(below, rows, streams[turn], pl.ds(below, rows))]
-                    else:
-                        parts = [
-                            (first_row, rows, streams[number * plan.cores + turn], slice(None))
-                            for number, (first_row, rows) in enumerate(stage.chunks)
-                        ]
-                    for first_row, rows, stream, window in parts:
-                        lane = lax.broadcasted_iota(jnp.int32, (plan.half, rows), 1) + first_row
-                        pick = jnp.where(lane == row, 1.0, 0.0).astype(jnp.bfloat16)
-                        both = jnp.dot(pick, stream[window, :], preferred_element_type=jnp.float32)
-                        key = key + both[:, : plan.width]
-                        value = value + both[:, plan.width :]
-                    place = pl.ds(pl.multiple_of(source_core * plan.half, plan.half), plan.half)
-                    keys[at, place, :] = key.astype(jnp.bfloat16)
-                    values[at, place, :] = value.astype(jnp.bfloat16)
-
-            offset = offset + (plan.half - taken) * live.astype(jnp.float32)
+
+            @pl.when(live & (rank >= stage.ranks[0]))
+            def _():
+                token = lax.broadcasted_iota(jnp.int32, (plan.half, SEL), 0) + base
+                same = jnp.where(listed == token, 1.0, 0.0)
+                ahead = jnp.sum(jnp.where(listed < token, 1.0, 0.0), axis=1, keepdims=True)
+                chosen = jnp.sum(same, axis=1, keepdims=True)
+                row = lax.broadcasted_iota(jnp.int32, (plan.half, 1), 0).astype(jnp.float32)
+                row = row + offset - ahead + first
+                row = jnp.where(chosen > 0.5, -1.0, row).astype(jnp.int32)
+                fresh_pick = same.astype(jnp.bfloat16)
+                key = jnp.dot(fresh_pick, fresh_key_ref[request, :SEL, :], preferred_element_type=jnp.float32)
+                value = jnp.dot(fresh_pick, fresh_value_ref[request, :SEL, :], preferred_element_type=jnp.float32)
+                below = jnp.max(offset.astype(jnp.int32)) // 16 * 16
+                below = pl.multiple_of(jnp.minimum(below, held - rows), 16)
+                lane = lax.broadcasted_iota(jnp.int32, (plan.half, rows), 1) + below
+                pick = jnp.where(lane == row, 1.0, 0.0).astype(jnp.bfloat16)
+                both = jnp.dot(pick, joined[turn, pl.ds(below, rows), :], preferred_element_type=jnp.float32)
+                at = rank - stage.ranks[0]
+                place = pl.ds(pl.multiple_of(source_core * plan.half, plan.half), plan.half)
+                keys[at, place, :] = (key + both[:, : plan.width]).astype(jnp.bfloat16)
+                values[at, place, :] = (value + both[:, plan.width :]).astype(jnp.bfloat16)
+                if stage.left:
+                    @pl.when(left_ref[0] > 0)
+                    def _():
+                        over = lax.broadcasted_iota(jnp.int32, (plan.half, plan.left_rows), 1) + plan.sent_rows
+                        extra = jnp.where(over == row, 1.0, 0.0).astype(jnp.bfloat16)
+                        more = jnp.dot(extra, joined[turn, held:, :], preferred_element_type=jnp.float32)
+                        more = more.astype(jnp.bfloat16)
+                        keys[at, place, :] += more[:, : plan.width]
+                        values[at, place, :] += more[:, plan.width :]
+
+            return offset + (plan.half - taken) * live.astype(jnp.float32)
+
+        lax.fori_loop(0, stage.ranks[-1] + 1, one_rank, jnp.zeros((1, 1), jnp.float32))
+        return unused
+
+    lax.fori_loop(0, plan.cores, one_turn, 0)
 
 
 def attend_kernel(plan, stage, *refs):
@@ -248,20 +266,20 @@
         del refs[:count]
         return taken
 
-    ids_ref, slot_ref, pos_ref, len_ref, _ = take(5)
+    ids_ref, slot_ref, pos_ref, len_ref, _, left_ref = take(6)
     column_ref, my_pos_ref, fresh_key_ref, fresh_value_ref = take(4)
     if stage.opening:
         (query_in,) = take(1)
     else:
         query, sizes = take(2)
         take(3)
-    streams = take(len(stage.chunks) * plan.cores)
+    streams = take((len(stage.chunks) + stage.left) * plan.cores)
     if stage.closing:
         (out_ref,) = take(1)
     total_ref, sums_ref, top_ref = take(3)
     if stage.opening:
         query, sizes = take(2)
-    keys, values, table = take(3)
+    keys, values, joined, table = take(4)
     request = pl.program_id(0)
     store = lax.axis_index("store")
     span = plan.half * plan.cores
@@ -275,7 +293,13 @@
         for rank in range(plan.capacity):
             table[2 * rank] = jnp.where(live[rank] > 0, owners[rank], -1)
             table[2 * rank + 1] = turns[rank] * SPAN
-        blend(plan, stage, table, my_pos_ref, fresh_key_ref, fresh_value_ref, streams, keys, values)
+        at = 0
+        for number in range(len(stage.chunks) + stage.left):
+            rows = streams[number * plan.cores].shape[0]
+            for turn in range(plan.cores):
+                joined[turn, at : at + rows, :] = streams[number * plan.cores + turn][...]
+            at += rows
+        blend(plan, stage, table, left_ref, my_pos_ref, fresh_key_ref, fresh_value_ref, joined, keys, values)
 
     def rows_of(tile):
         return pl.ds(pl.multiple_of(tile * TILE, 16), TILE)
@@ -437,7 +461,7 @@
         lax.fori_loop(0, last, finish, 0)
 
 
-def attend(plan, stage, state, arrays, fresh, ids, slots, my_pos, pos, pos_column, lengths):
+def attend(plan, stage, state, arrays, fresh, ids, slots, my_pos, pos, pos_column, lengths, left_over):
     fresh_query, fresh_keys, fresh_values = fresh
     req_dev = plan.req_dev
     row_block = lambda width: pl.BlockSpec((1, ROWS, width), lambda r, *_: (r, 0, 0))
@@ -445,7 +469,7 @@
     kept = pl.BlockSpec(memory_space=pltpu.VMEM)
     fresh_block = pl.BlockSpec((req_dev, ROWS, plan.width), lambda r, *s: (0, 0, s[4][0]))
     kv_block = jnp.reshape(plan.kv_block, (1,))
-    operands = [ids, slots, pos, lengths, kv_block, pos_column, my_pos, fresh_keys, fresh_values]
+    operands = [ids, slots, pos, lengths, kv_block, left_over, pos_column, my_pos, fresh_keys, fresh_values]
     specs = [row_block(1), whole(my_pos), fresh_block, fresh_block]
     aliases = {}
     stacked = (req_dev, plan.kv_used, plan.q_heads // plan.kv_used * ROWS, HD)
@@ -464,6 +488,8 @@
     specs += [whole(a) for a in arrays]
     span = plan.half * plan.cores
     scratch = [pltpu.VMEM((len(stage.ranks), span, plan.width), jnp.bfloat16)] * 2
+    joined_rows = sum(array.shape[0] for array in arrays) // plan.cores
+    scratch += [pltpu.VMEM((plan.cores, joined_rows, 2 * plan.width), jnp.bfloat16)]
     scratch += [pltpu.SMEM((2 * plan.capacity,), jnp.int32)]
     out_shape += [pltpu.VMEM(stacked, jnp.float32)] * 3
     out_specs += [kept] * 3
@@ -475,7 +501,7 @@
         functools.partial(attend_kernel, plan, stage),
         out_shape=out_shape,
         grid_spec=pltpu.PrefetchScalarGridSpec(
-            num_scalar_prefetch=5,
+            num_scalar_prefetch=6,
             grid=(req_dev,),
             in_specs=specs,
             out_specs=out_specs,
@@ -495,9 +521,30 @@
 
 
 class Stage:
-    def __init__(self, step, ranks, chunks, opening=False, closing=False):
-        self.step, self.ranks, self.chunks = step, ranks, chunks
-        self.opening, self.closing = opening, closing
+    def __init__(self, step, ranks, chunks, left):
+        self.step, self.ranks, self.chunks, self.left = step, ranks, chunks, left
+        self.opening = self.closing = False
+
+
+def most_live(plan, span_ids, span_slot, select_pos):
+    halves = CTX // plan.half
+    listed = (select_pos // plan.half)[:, :, None] == jnp.arange(halves, dtype=jnp.int32)
+    live = plan.half - jnp.sum(listed.astype(jnp.int32), axis=1)
+    spans = span_ids.reshape(plan.stores, plan.refs)
+    known = spans[:, :, None] == jnp.arange(span_slot.shape[0], dtype=jnp.int32)
+    owner = jnp.sum(jnp.where(known, span_slot // plan.ch_dev, 0), axis=2)
+    live = live.reshape(plan.stores, plan.refs, plan.cores)
+    theirs = owner[:, :, None] == jnp.arange(plan.stores, dtype=jnp.int32)
+    counts = jnp.sum(jnp.where(theirs[..., None], live[:, :, None, :], 0), axis=1)
+    most = jnp.max(counts).reshape(1)
+    groups = lax.axis_size("groups")
+    others = [
+        lax.ppermute(most, "groups", [(g, (g + turn) % groups) for g in range(groups)])
+        for turn in range(1, groups)
+    ]
+    for other in others:
+        most = jnp.maximum(most, other)
+    return most
 
 
 def body(
@@ -518,7 +565,7 @@
     steps = list(range(1, plan.stores))
     arrived = {}
     for step in steps + [0]:
-        chunks = plan.split if step == steps[-1] else plan.chunks
+        chunks = plan.chunks(step)
         own_ids = ids
         if step != steps[0]:
             own_ids, _ = lax.optimization_barrier((ids, before))
@@ -532,6 +579,29 @@
                 if step != 0 or turn != 0:
                     block = lax.ppermute(block, ("store", "sub"), plan.pairs(step, turn))
                 arrived[(step, chunk, turn)] = block
+    left, left_over = {}, jnp.zeros((1,), jnp.int32)
+    if plan.left_rows:
+        most = most_live(plan, span_ids, span_slot, select_pos)
+        left_over = (most > plan.sent_rows).astype(jnp.int32)
+
+        def send_left():
+            blocks = []
+            for step in steps:
+                rest = pack(
+                    plan, step, [(plan.sent_rows, plan.left_rows)], ids, span_slot, chosen, store_keys, store_values
+                )
+                for turn in range(plan.cores):
+                    blocks.append(lax.ppermute(rest[turn], ("store", "sub"), plan.pairs(step, turn)))
+            return tuple(blocks)
+
+        def nothing():
+            return tuple(
+                jnp.zeros((plan.left_rows, 2 * plan.width), jnp.bfloat16) for _ in steps for _ in range(plan.cores)
+            )
+
+        blocks = lax.cond(left_over[0] > 0, send_left, nothing)
+        for number, step in enumerate(steps):
+            left[step] = list(blocks[number * plan.cores : (number + 1) * plan.cores])
     my_pos = lax.dynamic_slice_in_dim(select_pos, store_index * plan.req_dev, plan.req_dev, 0)
     lengths = lax.dynamic_slice_in_dim(ask_len, store_index * plan.req_dev, plan.req_dev, 0)
     asked = jnp.broadcast_to(CTX + jnp.arange(QLEN, dtype=jnp.int32), (plan.req_dev, QLEN))
@@ -539,13 +609,18 @@
     pos_column = pos[:, :, None]
     pos = pos.reshape(-1)
     all_ranks = list(range(plan.capacity))
-    stages = [Stage(step, all_ranks, plan.chunks) for step in [0] + steps]
+    stages = []
+    for step in [0] + steps:
+        chunks = plan.chunks(step)
+        groups = [all_ranks]
+        if len(chunks) == plan.capacity:
+            groups = [[rank] for rank in all_ranks]
+        elif len(chunks) == 2:
+            groups = [all_ranks[:-1], all_ranks[-1:]]
+        for number, ranks in enumerate(groups):
+            remains = step != 0 and plan.left_rows > 0 and ranks[-1] == all_ranks[-1]
+            stages.append(Stage(step, ranks, chunks[: number + 1], int(remains)))
     stages[0].opening = True
-    if len(plan.split) > 1:
-        stages[-1:] = [
-            Stage(steps[-1], all_ranks[:-1], plan.split[:-1]),
-            Stage(steps[-1], all_ranks[-1:], plan.split),
-        ]
     stages[-1].closing = True
     state = None
     for stage in stages:
@@ -554,9 +629,11 @@
             for chunk in range(len(stage.chunks))
             for turn in range(plan.cores)
         ]
+        if stage.left:
+            arrays += left[stage.step]
         state = attend(
             plan, stage, state, arrays, (fresh_query, fresh_keys, fresh_values), ids, span_slot,
-            my_pos, pos, pos_column, lengths,
+            my_pos, pos, pos_column, lengths, left_over,
         )
     return state
 

time: 1030 us -> 1050 us (1.019)
    pallas_call x5 -> x7, Pallas kernels: 988 us -> 993 us  [attend(): pl.pallas_call(functools.partial(attend_kernel, plan, stage), out_shape=o...]
  transfers between devices with their start and end apart: 9 -> 14, of which waited for: 0 -> 0; matrix products, arithmetic and copies ran while one was open for 0% -> 0% of each run, Pallas kernels for 88% -> 88%
where the time goes in v1:
time: 1050 us
  Pallas kernels  1010 us (96%)
  starting transfers between devices  21.4 us (2%)
  local copies, waits for them, and re-layouts  11 us (1%)
    pallas_call x7, Pallas kernels, attend(): pl.pallas_call(functools.partial(attend_kernel, plan, stage), out_shape=o...  993 us
  transfers between devices with their start and end apart: 14, of which 0 were waited for; matrix products, arithmetic and copies ran while one was open for 0% of the time, Pallas kernels for 88%

profile of v1, /device:TPU:0, one launch (start us, length us, event | category | flops | bytes accessed | tf_op | source)
XLA Modules:
  0.0 1046.9 jit_solution(10624264602955438752)
XLA Ops:
  0.0 0.8 and_select_fusion
  4.3 3.0 collective-permute-start.6
  8.1 0.8 copy.62
  8.9 4.6 shard_map.91
  13.5 4.5 shard_map.92
  18.1 3.6 shard_map.93
  21.7 4.6 shard_map.94
  27.4 3.8 conditional.1
  31.3 1.6 collective-permute-start.8
  32.9 2.6 collective-permute-start.10
  36.9 0.9 copy-done.2
  37.8 3.4 collective-permute-start.12
  41.3 1.1 copy-done.3
  42.4 1.1 copy-done.4
  43.5 268.0 %shard_map.95 = (f32[2,2,4224,128]{3,2,1,0:T(8,128)S(1)}, f32[2,2,4224,128]{3,2,1,0:T(8,128)S(1)}, f32[2,2,4224,128]{3,2,1,0:T(8,128)S(1)}, bf16[2,2,4224,128]{3,2,1,0:T(8,128)(2,1)S(1)}, f32[2,2,48,128]{3,2,1,0:T(8,128)S(1)}) custom-call(s32[48]{0:T(128)S(1)} %reshape.35.ids_ref.refs_0_, s32[32]{0:T(128)S(1)} %copy-done.5, s32[1056]{0:T(1024)S(1)} %reshape.36.refs_2_, ...), custom_call_target="tpu_custom_call" | custom-call | flops 6643777536 | bytes 8650752 | tf_op jit(solution)/shard_map/pallas_call | solution.py:500
  312.1 2.2 collective-permute-start.11
  314.3 238.3 %shard_map.96 = (f32[2,2,4224,128]{3,2,1,0:T(8,128)S(1)}, f32[2,2,4224,128]{3,2,1,0:T(8,128)S(1)}, f32[2,2,4224,128]{3,2,1,0:T(8,128)S(1)}) custom-call(s32[48]{0:T(128)S(1)} %reshape.35.ids_ref.refs_0_, s32[32]{0:T(128)S(1)} %copy-done.5, s32[1056]{0:T(1024)S(1)} %reshape.36.refs_2_, ...), custom_call_target="tpu_custom_call", output_to_operand_aliasing={{0}: (12, {}), {1}: (13, {}), {2}: (14, {})} | custom-call | flops 6643777536 | bytes 8650752 | tf_op jit(solution)/shard_map/pallas_call | solution.py:500
  553.0 3.4 collective-permute-start.15
  556.4 159.4 %shard_map.97 = (f32[2,2,4224,128]{3,2,1,0:T(8,128)S(1)}, f32[2,2,4224,128]{3,2,1,0:T(8,128)S(1)}, f32[2,2,4224,128]{3,2,1,0:T(8,128)S(1)}) custom-call(s32[48]{0:T(128)S(1)} %reshape.35.ids_ref.refs_0_, s32[32]{0:T(128)S(1)} %copy-done.5, s32[1056]{0:T(1024)S(1)} %reshape.36.refs_2_, ...), custom_call_target="tpu_custom_call", output_to_operand_aliasing={{0}: (12, {}), {1}: (13, {}), {2}: (14, {})} | custom-call | flops 4429185024 | bytes 8650752 | tf_op jit(solution)/shard_map/pallas_call | solution.py:500
  716.3 3.0 collective-permute-start.17
  719.3 81.5 %shard_map.98 = (f32[2,2,4224,128]{3,2,1,0:T(8,128)S(1)}, f32[2,2,4224,128]{3,2,1,0:T(8,128)S(1)}, f32[2,2,4224,128]{3,2,1,0:T(8,128)S(1)}) custom-call(s32[48]{0:T(128)S(1)} %reshape.35.ids_ref.refs_0_, s32[32]{0:T(128)S(1)} %copy-done.5, s32[1056]{0:T(1024)S(1)} %reshape.36.refs_2_, ...), custom_call_target="tpu_custom_call", output_to_operand_aliasing={{0}: (12, {}), {1}: (13, {}), {2}: (14, {})} | custom-call | flops 2214592512 | bytes 8650752 | tf_op jit(solution)/shard_map/pallas_call | solution.py:500
  801.5 80.5 %shard_map.99 = (f32[2,2,4224,128]{3,2,1,0:T(8,128)S(1)}, f32[2,2,4224,128]{3,2,1,0:T(8,128)S(1)}, f32[2,2,4224,128]{3,2,1,0:T(8,128)S(1)}) custom-call(s32[48]{0:T(128)S(1)} %reshape.35.ids_ref.refs_0_, s32[32]{0:T(128)S(1)} %copy-done.5, s32[1056]{0:T(1024)S(1)} %reshape.36.refs_2_, ...), custom_call_target="tpu_custom_call", output_to_operand_aliasing={{0}: (12, {}), {1}: (13, {}), {2}: (14, {})} | custom-call | flops 2214592512 | bytes 8650752 | tf_op jit(solution)/shard_map/pallas_call | solution.py:500
  882.0 80.9 %shard_map.100 = (f32[2,2,4224,128]{3,2,1,0:T(8,128)S(1)}, f32[2,2,4224,128]{3,2,1,0:T(8,128)S(1)}, f32[2,2,4224,128]{3,2,1,0:T(8,128)S(1)}) custom-call(s32[48]{0:T(128)S(1)} %reshape.35.ids_ref.refs_0_, s32[32]{0:T(128)S(1)} %copy-done.5, s32[1056]{0:T(1024)S(1)} %reshape.36.refs_2_, ...), custom_call_target="tpu_custom_call", output_to_operand_aliasing={{0}: (12, {}), {1}: (13, {}), {2}: (14, {})} | custom-call | flops 2214592512 | bytes 8650752 | tf_op jit(solution)/shard_map/pallas_call | solution.py:500
  962.9 84.0 %shard_map.101 = (bf16[2,528,2048]{2,1,0:T(8,128)(2,1)}, f32[2,2,4224,128]{3,2,1,0:T(8,128)S(1)}, f32[2,2,4224,128]{3,2,1,0:T(8,128)S(1)}, f32[2,2,4224,128]{3,2,1,0:T(8,128)S(1)}) custom-call(s32[48]{0:T(128)S(1)} %reshape.35.ids_ref.refs_0_, s32[32]{0:T(128)S(1)} %copy-done.5, ...), custom_call_target="tpu_custom_call", output_to_operand_aliasing={{1}: (12, {}), {2}: (13, {}), {3}: (14, {})} | custom-call | flops 2214592512 | bytes 8650752 | tf_op jit(solution)/shard_map/pallas_call | solution.py:500
  (76 shorter events, 11.5 us)
Async XLA Ops:
  0.0 18.1 %copy-start.6 = (bf16[8,256,512]{2,1,0:T(8,128)(2,1)S(1)}, bf16[8,256,512]{2,1,0:T(8,128)(2,1)}, u32[]{:S(2)}) copy-start(bf16[8,256,512]{2,1,0:T(8,128)(2,1)} %keys_ref.7) | copy-start | bytes 6291460
  4.3 22.0 %collective-permute-start.6 = (s32[1]{0:T(128)}, s32[1]{0:T(128)}, u32[]{:S(2)}, u32[]{:S(2)}) collective-permute-start(s32[1]{0:T(128)} %bitcast.1), channel_id=1, source_target_pairs={{0,16},{16,0},{1,17},{17,1},{2,18},{18,2},{3,19},{19,3},{4,20},{20... | collective-permute-start | bytes 20 | tf_op jit(solution)/shard_map/ppermute | solution.py:542
  21.6 19.6 %copy-start = (bf16[2,528,512]{2,1,0:T(8,128)(2,1)S(1)}, bf16[2,528,512]{2,1,0:T(8,128)(2,1)}, u32[]{:S(2)}) copy-start(bf16[2,528,512]{2,1,0:T(8,128)(2,1)} %refs_8_.13) | copy-start | bytes 3244036
  21.7 19.6 %copy-start.1 = (bf16[2,528,512]{2,1,0:T(8,128)(2,1)S(1)}, bf16[2,528,512]{2,1,0:T(8,128)(2,1)}, u32[]{:S(2)}) copy-start(bf16[2,528,512]{2,1,0:T(8,128)(2,1)} %refs_9_.13) | copy-start | bytes 3244036
  31.3 5.6 collective-permute-start.7
  31.3 280.8 %collective-permute-start.8 = (bf16[688,512]{1,0:T(8,128)(2,1)}, bf16[688,512]{1,0:T(8,128)(2,1)}, u32[]{:S(2)}, u32[]{:S(2)}) collective-permute-start(bf16[688,512]{1,0:T(8,128)(2,1)} %get-tuple-element.70), channel_id=1, source_target_pairs={{0,4},{1,5},{4,0},{5,1},{8,12},{9,13},{12,8},{13,9},{2,6},{3,7},{6... | collective-permute-start | bytes 2113544 | tf_op jit(solution)/shard_map/ppermute | solution.py:580
  32.9 520.1 %collective-permute-start.10 = (bf16[512,512]{1,0:T(8,128)(2,1)}, bf16[512,512]{1,0:T(8,128)(2,1)}, u32[]{:S(2)}, u32[]{:S(2)}) collective-permute-start(bf16[512,512]{1,0:T(8,128)(2,1)} %get-tuple-element.72), channel_id=1, source_target_pairs={{0,8},{1,9},{4,12},{5,13},{8,0},{9,1},{12,4},{13,5},{2,10},{3,11},... | collective-permute-start | bytes 1572872 | tf_op jit(solution)/shard_map/ppermute | solution.py:580
  35.5 766.0 %collective-permute-start.14 = (bf16[256,512]{1,0:T(8,128)(2,1)}, bf16[256,512]{1,0:T(8,128)(2,1)}, u32[]{:S(2)}, u32[]{:S(2)}) collective-permute-start(bf16[256,512]{1,0:T(8,128)(2,1)} %get-tuple-element.74), channel_id=1, source_target_pairs={{0,12},{1,13},{4,8},{5,9},{8,4},{9,5},{12,0},{13,1},{2,14},{3,15},... | collective-permute-start | bytes 786440 | tf_op jit(solution)/shard_map/ppermute | solution.py:580
  35.7 275.8 %collective-permute-start.9 = (bf16[688,512]{1,0:T(8,128)(2,1)}, bf16[688,512]{1,0:T(8,128)(2,1)}, u32[]{:S(2)}, u32[]{:S(2)}) collective-permute-start(bf16[688,512]{1,0:T(8,128)(2,1)} %get-tuple-element.83), channel_id=1, source_target_pairs={{0,5},{1,4},{4,1},{5,0},{8,13},{9,12},{12,9},{13,8},{2,7},{3,6},{6... | collective-permute-start | bytes 2113544 | tf_op jit(solution)/shard_map/ppermute | solution.py:580
  37.8 678.0 %collective-permute-start.12 = (bf16[176,512]{1,0:T(8,128)(2,1)}, bf16[176,512]{1,0:T(8,128)(2,1)S(1)}, u32[]{:S(2)}, u32[]{:S(2)}) collective-permute-start(bf16[176,512]{1,0:T(8,128)(2,1)} %get-tuple-element.93), channel_id=1, source_target_pairs={{0,8},{1,9},{4,12},{5,13},{8,0},{9,1},{12,4},{13,5},{2,10},{3,11},... | collective-permute-start | bytes 540680 | tf_op jit(solution)/shard_map/ppermute | solution.py:580
  43.5 268.0 %copy-start.13 = (bf16[176,512]{1,0:T(8,128)(2,1)S(1)}, bf16[176,512]{1,0:T(8,128)(2,1)}, u32[]{:S(2)}) copy-start(bf16[176,512]{1,0:T(8,128)(2,1)} %get-tuple-element.94) | copy-start | bytes 540676
  43.5 268.5 %copy-start.7 = (bf16[512,512]{1,0:T(8,128)(2,1)S(1)}, bf16[512,512]{1,0:T(8,128)(2,1)}, u32[]{:S(2)}) copy-start(bf16[512,512]{1,0:T(8,128)(2,1)} %get-tuple-element.89) | copy-start | bytes 1572868
  311.5 404.8 %collective-permute-start.13 = (bf16[176,512]{1,0:T(8,128)(2,1)S(1)}, bf16[176,512]{1,0:T(8,128)(2,1)S(1)}, u32[]{:S(2)}, u32[]{:S(2)}) collective-permute-start(bf16[176,512]{1,0:T(8,128)(2,1)S(1)} %copy-done.13), channel_id=1, source_target_pairs={{0,9},{1,8},{4,13},{5,12},{8,1},{9,0},{12,5},{13,4},{2,11},{3,10},... | collective-permute-start | bytes 540680 | tf_op jit(solution)/shard_map/ppermute | solution.py:580
  312.1 240.5 %collective-permute-start.11 = (bf16[512,512]{1,0:T(8,128)(2,1)S(1)}, bf16[512,512]{1,0:T(8,128)(2,1)S(1)}, u32[]{:S(2)}, u32[]{:S(2)}) collective-permute-start(bf16[512,512]{1,0:T(8,128)(2,1)S(1)} %copy-done.7), channel_id=1, source_target_pairs={{0,9},{1,8},{4,13},{5,12},{8,1},{9,0},{12,5},{13,4},{2,11},{3,10},... | collective-permute-start | bytes 1572872 | tf_op jit(solution)/shard_map/ppermute | solution.py:580
  314.3 238.3 %copy-start.12 = (bf16[176,512]{1,0:T(8,128)(2,1)S(1)}, bf16[176,512]{1,0:T(8,128)(2,1)}, u32[]{:S(2)}) copy-start(bf16[176,512]{1,0:T(8,128)(2,1)} %get-tuple-element.109) | copy-start | bytes 540676
  314.3 238.7 %copy-start.10 = (bf16[256,512]{1,0:T(8,128)(2,1)S(1)}, bf16[256,512]{1,0:T(8,128)(2,1)}, u32[]{:S(2)}) copy-start(bf16[256,512]{1,0:T(8,128)(2,1)} %get-tuple-element.100) | copy-start | bytes 786436
  552.6 410.3 %collective-permute-start.18 = (bf16[176,512]{1,0:T(8,128)(2,1)S(1)}, bf16[176,512]{1,0:T(8,128)(2,1)S(1)}, u32[]{:S(2)}, u32[]{:S(2)}) collective-permute-start(bf16[176,512]{1,0:T(8,128)(2,1)S(1)} %copy-done.12), channel_id=1, source_target_pairs={{0,12},{1,13},{4,8},{5,9},{8,4},{9,5},{12,0},{13,1},{2,14},{3,15},... | collective-permute-start | bytes 540680 | tf_op jit(solution)/shard_map/ppermute | solution.py:580
  553.0 247.9 %collective-permute-start.15 = (bf16[256,512]{1,0:T(8,128)(2,1)S(1)}, bf16[256,512]{1,0:T(8,128)(2,1)S(1)}, u32[]{:S(2)}, u32[]{:S(2)}) collective-permute-start(bf16[256,512]{1,0:T(8,128)(2,1)S(1)} %copy-done.10), channel_id=1, source_target_pairs={{0,13},{1,12},{4,9},{5,8},{8,5},{9,4},{12,1},{13,0},{2,15},{3,14},... | collective-permute-start | bytes 786440 | tf_op jit(solution)/shard_map/ppermute | solution.py:580
  556.4 159.5 %copy-start.9 = (bf16[256,512]{1,0:T(8,128)(2,1)S(1)}, bf16[256,512]{1,0:T(8,128)(2,1)}, u32[]{:S(2)}) copy-start(bf16[256,512]{1,0:T(8,128)(2,1)} %get-tuple-element.104) | copy-start | bytes 786436
  556.4 159.9 %copy-start.8 = (bf16[256,512]{1,0:T(8,128)(2,1)S(1)}, bf16[256,512]{1,0:T(8,128)(2,1)}, u32[]{:S(2)}) copy-start(bf16[256,512]{1,0:T(8,128)(2,1)} %get-tuple-element.105) | copy-start | bytes 786436
  715.9 166.1 %collective-permute-start.16 = (bf16[256,512]{1,0:T(8,128)(2,1)S(1)}, bf16[256,512]{1,0:T(8,128)(2,1)S(1)}, u32[]{:S(2)}, u32[]{:S(2)}) collective-permute-start(bf16[256,512]{1,0:T(8,128)(2,1)S(1)} %copy-done.9), channel_id=1, source_target_pairs={{0,12},{1,13},{4,8},{5,9},{8,4},{9,5},{12,0},{13,1},{2,14},{3,15},... | collective-permute-start | bytes 786440 | tf_op jit(solution)/shard_map/ppermute | solution.py:580
  716.3 165.7 %collective-permute-start.17 = (bf16[256,512]{1,0:T(8,128)(2,1)S(1)}, bf16[256,512]{1,0:T(8,128)(2,1)S(1)}, u32[]{:S(2)}, u32[]{:S(2)}) collective-permute-start(bf16[256,512]{1,0:T(8,128)(2,1)S(1)} %copy-done.8), channel_id=1, source_target_pairs={{0,13},{1,12},{4,9},{5,8},{8,5},{9,4},{12,1},{13,0},{2,15},{3,14},... | collective-permute-start | bytes 786440 | tf_op jit(solution)/shard_map/ppermute | solution.py:580
  719.3 81.5 %copy-start.11 = (bf16[176,512]{1,0:T(8,128)(2,1)S(1)}, bf16[176,512]{1,0:T(8,128)(2,1)}, u32[]{:S(2)}) copy-start(bf16[176,512]{1,0:T(8,128)(2,1)} %get-tuple-element.110) | copy-start | bytes 540676
  800.9 162.0 %collective-permute-start.19 = (bf16[176,512]{1,0:T(8,128)(2,1)S(1)}, bf16[176,512]{1,0:T(8,128)(2,1)S(1)}, u32[]{:S(2)}, u32[]{:S(2)}) collective-permute-start(bf16[176,512]{1,0:T(8,128)(2,1)S(1)} %copy-done.11), channel_id=1, source_target_pairs={{0,13},{1,12},{4,9},{5,8},{8,5},{9,4},{12,1},{13,0},{2,15},{3,14},... | collective-permute-start | bytes 540680 | tf_op jit(solution)/shard_map/ppermute | solution.py:580
  (5 other events, 36.1 us)
